TPU v7x, 512 devices: a whole 4x8x8 slice. The times are simulated.
512 devices in a mesh: band: 32 (over z_hi, x, core), chan: 16 (over y, z_lo).
Axes of the slice: x: 4, y: 8, z: 8 (z_hi: 4, z_lo: 2; z = z_hi * 2 + z_lo), core: 2. Of those that a mesh axis runs over, the one named last changes fastest.
Arguments:
- image: bfloat16 [512, 128, 512], P('chan', 'band'), may hold values from -6 to 6
- filters: bfloat16 [9, 512, 512], P(None, None, 'chan'), may hold values from -0.09375 to 0.09375
- bias: bfloat16 [512], P('chan'), may hold values from -3 to 3
- upstream: bfloat16 [512, 128, 512], P('chan', 'band'), may hold values from -6 to 6
Outputs:
- features: bfloat16 [512, 128, 512], P('chan', 'band')
- image_grad: bfloat16 [512, 128, 512], P('chan', 'band')
All inputs are finite; a program needn't handle non-finite values.
Results may differ from a plain program's by a relative error of at most 0.001.
Values may be sent and summed in bfloat16 or wider, within the bound.
A program may use at most 64 MiB of HBM per device.

v0:
```python
import jax
import jax.numpy as jnp
from jax import lax
from jax.sharding import PartitionSpec as P


def with_halo(value, sides, width):
    for axis, dim in sides:
        size, length = (lax.axis_size(axis), value.shape[dim])
        up = [(i, (i + 1) % size) for i in range(size - 1)]
        down = [(j, i) for i, j in up]
        last = lax.slice_in_dim(value, length - width, length, axis=dim)
        first = lax.slice_in_dim(value, 0, width, axis=dim)
        before = lax.ppermute(last, axis, up)
        after = lax.ppermute(first, axis, down)
        value = jnp.concatenate([before, value, after], axis=dim)
    return value


def tap_forward(weights, source, row_count, col_count):
    result = None
    for tap_row in range(3):
        for tap_col in range(3):
            term = jnp.einsum(
                "oi,irc->orc",
                weights[tap_row * 3 + tap_col],
                source[:, tap_row : tap_row + row_count, tap_col : tap_col + col_count],
                preferred_element_type=jnp.float32,
            )
            result = term if result is None else result + term
    return result


def tap_backward(weights, source, row_count, col_count):
    result = None
    for tap_row in range(3):
        for tap_col in range(3):
            term = jnp.einsum(
                "oi,orc->irc",
                weights[tap_row * 3 + tap_col],
                source[
                    :, 2 - tap_row : 2 - tap_row + row_count, 2 - tap_col : 2 - tap_col + col_count
                ],
                preferred_element_type=jnp.float32,
            )
            result = term if result is None else result + term
    return result


def per_device(image, filters, bias, upstream):
    row_count = image.shape[1]
    col_count = image.shape[2]
    stacked = jnp.stack([image, upstream])
    with_rims = with_halo(stacked, (("band", 2),), 1)
    padded = jnp.pad(with_rims, ((0, 0), (0, 0), (0, 0), (1, 1)))
    outward = lax.all_to_all(filters, "chan", split_axis=1, concat_axis=2, tiled=True)
    w_part = outward
    forward_sum = tap_forward(
        w_part, lax.all_gather(padded[0], "chan", axis=0, tiled=True), row_count, col_count
    )
    w_part = filters
    grad_sum = tap_backward(
        w_part, lax.all_gather(padded[1], "chan", axis=0, tiled=True), row_count, col_count
    )
    features = (forward_sum + bias.astype(jnp.float32)[:, None, None]).astype(jnp.bfloat16)
    image_grad = grad_sum.astype(jnp.bfloat16)
    return (features, image_grad)


def solution(mesh):
    return jax.shard_map(
        per_device,
        mesh=mesh,
        in_specs=(
            P("chan", "band", None),
            P(None, None, "chan"),
            P("chan"),
            P("chan", "band", None),
        ),
        out_specs=(P("chan", "band", None), P("chan", "band", None)),
        check_vma=False,
    )
```

profile of v0, /device:TPU:18, one launch (start us, length us, event | category | flops | bytes accessed | tf_op | source)
XLA Modules:
  0.0 245.0 jit_solution(1787459723346832427)
XLA Ops:
  7.2 1.0 copy_bitcast_fusion.1
  8.3 1.9 collective-permute-start.1
  10.2 2.4 collective-permute-start
  12.6 3.2 %collective-permute-done = bf16[2,32,1,512]{3,1,2,0:T(8,128)(2,1)S(1)} collective-permute-done((bf16[2,32,1,512]{3,1,2,0:T(8,128)(2,1)S(1)}, bf16[2,32,1,512]{3,1,2,0:T(8,128)(2,1)S(1)}, u32[]{:S(2)}, u32[]{:S(2)}) %collective-permute-start) | collective-permute-done | bytes 65568 | tf_op jit(solution)/shard_map/ppermute | solution.py:14
  16.1 0.9 fusion.122
  17.7 2.0 copy.13
  19.7 2.0 reshape.52
  21.7 9.3 %all-to-all-start = ((bf16[16,2,4608]{2,1,0:T(2,128)(2,1)}), bf16[16,2,4608]{2,1,0:T(2,128)(2,1)S(1)}, u32[]{:S(2)}, u32[]{:S(2)}) async-start(bf16[16,2,4608]{2,1,0:T(2,128)(2,1)} %reshape.52), calls=%async_computation | async-start | bytes 589824 | tf_op jit(solution)/shard_map/all_to_all | solution.py:56
  31.0 10.4 %all-to-all-done = bf16[16,2,4608]{2,1,0:T(2,128)(2,1)S(1)} async-done(((bf16[16,2,4608]{2,1,0:T(2,128)(2,1)}), bf16[16,2,4608]{2,1,0:T(2,128)(2,1)S(1)}, u32[]{:S(2)}, u32[]{:S(2)}) %all-to-all-start) | async-done | bytes 294944 | tf_op jit(solution)/shard_map/all_to_all | solution.py:56
  41.4 1.4 reshape.53
  42.7 0.8 copy.20
  45.2 76.4 %all-gather.7.cloned.1.call-done = bf16[1,512,6,514]{3,1,2,0:T(8,128)(2,1)} async-done(((bf16[1,32,6,514]{3,1,2,0:T(8,128)(2,1)}), bf16[1,512,6,514]{3,1,2,0:T(8,128)(2,1)}) %all-gather.7.cloned.1.call-update) | async-done | bytes 3158032 | tf_op jit(solution)/shard_map/all_gather | solution.py:63
  121.6 2.2 fusion
  123.8 2.5 %fusion.2 = f32[4,512,32]{1,2,0:T(8,128)S(1)} fusion(bf16[512,6,514]{2,0,1:T(8,128)(2,1)} %bitcast.80, bf16[9,512,32]{1,2,0:T(8,128)(2,1)S(1)} %copy-done.3), kind=kOutput, calls=%fused_computation.2 | convolution fusion | flops 67108864 | bytes 2392064 | tf_op jit(solution)/shard_map/oi,orc->irc/dot_general | solution.py:38
  127.6 0.8 fusion.8
  130.4 94.7 %all-gather.5.cloned.1.call-done = bf16[1,512,6,514]{3,1,2,0:T(8,128)(2,1)} async-done(((bf16[1,32,6,514]{3,1,2,0:T(8,128)(2,1)}), bf16[1,512,6,514]{3,1,2,0:T(8,128)(2,1)}) %all-gather.5.cloned.1.call-update) | async-done | bytes 3158032 | tf_op jit(solution)/shard_map/all_gather | solution.py:59
  225.1 2.7 %fusion.18 = f32[4,512,32]{1,2,0:T(8,128)S(1)} fusion(bf16[32,512,1]{1,0,2:T(8,128)(2,1)S(1)} %reshape.33, bf16[512,6,514]{2,0,1:T(8,128)(2,1)} %bitcast.88), kind=kOutput, calls=%fused_computation.18 | convolution fusion | flops 67108864 | bytes 2392064 | tf_op jit(solution)/shard_map/oi,irc->orc/dot_general | solution.py:24
  227.8 2.5 %fusion.20 = f32[4,512,32]{1,2,0:T(8,128)S(1)} fusion(bf16[32,512,1]{1,0,2:T(8,128)(2,1)S(1)} %reshape.32, bf16[512,6,514]{2,0,1:T(8,128)(2,1)} %bitcast.89), kind=kOutput, calls=%fused_computation.20 | convolution fusion | flops 67108864 | bytes 2392064 | tf_op jit(solution)/shard_map/oi,irc->orc/dot_general | solution.py:24
  230.8 0.8 fusion.24
  231.6 0.8 fusion.26
  232.8 0.8 fusion.30
  233.6 0.8 fusion.32
  235.7 0.9 copy-done.1
  236.6 0.8 fusion.96
  (37 shorter events, 8.9 us)
Async XLA Ops:
  7.2 10.6 %copy-start.3 = (bf16[9,512,32]{1,2,0:T(8,128)(2,1)S(1)}, bf16[9,512,32]{1,2,0:T(8,128)(2,1)}, u32[]{:S(2)}) copy-start(bf16[9,512,32]{1,2,0:T(8,128)(2,1)} %param.5) | copy-start | bytes 884740
  7.2 114.4 %all-gather.7.cloned.1.call-start = ((), (), s32[]{:S(2)}) async-start(), calls=%async_computation.2 | async-start | bytes 4177920 | tf_op jit(solution)/shard_map/all_gather | solution.py:63
  8.3 4.3 %collective-permute-start.1 = (bf16[2,32,1,512]{3,1,2,0:T(8,128)(2,1)S(1)}, bf16[2,32,1,512]{3,1,2,0:T(8,128)(2,1)S(1)}, u32[]{:S(2)}, u32[]{:S(2)}) collective-permute-start(bf16[2,32,1,512]{3,1,2,0:T(8,128)(2,1)S(1)} %get-tuple-element.18), channel_id=1, source_target_pairs={{16,0},{32,16},{48,32},{64,48},{80,64},{96,80},{112,96},{128,112},... | collective-permute-start | bytes 196616 | tf_op jit(solution)/shard_map/ppermute | solution.py:15
  10.2 5.6 %collective-permute-start = (bf16[2,32,1,512]{3,1,2,0:T(8,128)(2,1)S(1)}, bf16[2,32,1,512]{3,1,2,0:T(8,128)(2,1)S(1)}, u32[]{:S(2)}, u32[]{:S(2)}) collective-permute-start(bf16[2,32,1,512]{3,1,2,0:T(8,128)(2,1)S(1)} %get-tuple-element.17), channel_id=1, source_target_pairs={{0,16},{16,32},{32,48},{48,64},{64,80},{80,96},{96,112},{112,128},... | collective-permute-start | bytes 196616 | tf_op jit(solution)/shard_map/ppermute | solution.py:14
  17.0 208.1 %all-gather.5.cloned.1.call-start = ((), (), s32[]{:S(2)}) async-start(), calls=%async_computation.1 | async-start | bytes 4177920 | tf_op jit(solution)/shard_map/all_gather | solution.py:59
  17.7 13.2 %copy-start.4 = (bf16[32]{0:T(256)(128)(2,1)S(1)}, bf16[32]{0:T(256)(128)(2,1)}, u32[]{:S(2)}) copy-start(bf16[32]{0:T(256)(128)(2,1)} %param.6) | copy-start | bytes 196
  21.7 19.7 %all-to-all-start = ((bf16[16,2,4608]{2,1,0:T(2,128)(2,1)}), bf16[16,2,4608]{2,1,0:T(2,128)(2,1)S(1)}, u32[]{:S(2)}, u32[]{:S(2)}) async-start(bf16[16,2,4608]{2,1,0:T(2,128)(2,1)} %reshape.52), calls=%async_computation | async-start | bytes 589824 | tf_op jit(solution)/shard_map/all_to_all | solution.py:56
  121.6 4.7 %copy-start = (bf16[1,512,6,514]{3,1,2,0:T(8,128)(2,1)S(1)}, bf16[1,512,6,514]{3,1,2,0:T(8,128)(2,1)}, u32[]{:S(2)}) copy-start(bf16[1,512,6,514]{3,1,2,0:T(8,128)(2,1)} %all-gather.7.cloned.1.call-done) | copy-start | bytes 9474052
  225.1 5.2 %copy-start.2 = (bf16[1,512,6,514]{3,1,2,0:T(8,128)(2,1)S(1)}, bf16[1,512,6,514]{3,1,2,0:T(8,128)(2,1)}, u32[]{:S(2)}) copy-start(bf16[1,512,6,514]{3,1,2,0:T(8,128)(2,1)} %all-gather.5.cloned.1.call-done) | copy-start | bytes 9474052
  234.4 2.2 copy-start.1
Sparse Core Ops, SparseCore 0:
  17.1 104.4 all-gather.6
  123.7 101.3 all-gather.4
where the time goes:
time: 245 us
  waiting for transfers between devices  185 us (76%)
  matrix products  19.4 us (8%)
  between operations  14.2 us (6%)
  starting transfers between devices  13.7 us (6%)
  local copies, waits for them, and re-layouts  12.1 us (5%)
    all_gather x1, waiting for transfers between devices, per_device(): lax.all_gather(padded[0], 'chan', axis=0, tiled=True)  94.7 us
    all_gather x1, waiting for transfers between devices, per_device(): lax.all_gather(padded[1], 'chan', axis=0, tiled=True)  76.4 us
    all_to_all x1, waiting for transfers between devices, per_device(): lax.all_to_all(filters, 'chan', split_axis=1, concat_axis=2, tiled=True)  10.4 us
    dot_general x9, matrix products, tap_forward(): jnp.einsum('oi,irc->orc', weights[tap_row * 3 + tap_col], source[:, tap_r...  9.83 us
    dot_general x9, matrix products, tap_backward(): jnp.einsum('oi,orc->irc', weights[tap_row * 3 + tap_col], source[:, 2 - t...  9.61 us
    all_to_all x1, starting transfers between devices, per_device(): lax.all_to_all(filters, 'chan', split_axis=1, concat_axis=2, tiled=True)  9.26 us
    unnamed x15, local copies, waits for them, and re-layouts  7.71 us
  transfers between devices with their start and end apart: 5, of which 4 were waited for; matrix products, arithmetic and copies ran while one was open for 7% of the time, Pallas kernels for 0%

commit v1 on v0

--- a/solution.py
+++ b/solution.py
@@ -55,9 +55,20 @@
     padded = jnp.pad(with_rims, ((0, 0), (0, 0), (0, 0), (1, 1)))
     outward = lax.all_to_all(filters, "chan", split_axis=1, concat_axis=2, tiled=True)
     w_part = outward
-    forward_sum = tap_forward(
-        w_part, lax.all_gather(padded[0], "chan", axis=0, tiled=True), row_count, col_count
-    )
+
+    def _keep_up_cubes(values, bus_axis, along_dim):
+        local_next = jnp.concatenate(
+            lax.all_to_all(
+                jnp.stack([values for _ in range(lax.axis_size(bus_axis))]),
+                axis_name=bus_axis,
+                split_axis=0,
+                concat_axis=0,
+            ),
+            axis=along_dim,
+        )
+        return local_next
+
+    forward_sum = tap_forward(w_part, _keep_up_cubes(padded[0], "chan", 0), row_count, col_count)
     w_part = filters
     grad_sum = tap_backward(
         w_part, lax.all_gather(padded[1], "chan", axis=0, tiled=True), row_count, col_count

time: 245 us -> 223 us (0.910)
  the two profiles are of different devices: /device:TPU:18 before, /device:TPU:90 now
where the time goes in v1:
time: 223 us
  waiting for transfers between devices  145 us (65%)
  blocking collectives  18.7 us (8%)
  local copies, waits for them, and re-layouts  16.3 us (7%)
  matrix products  15.9 us (7%)
  between operations  14.2 us (6%)
  starting transfers between devices  12.9 us (6%)
    all_gather x1, waiting for transfers between devices, per_device(): lax.all_gather(padded[1], 'chan', axis=0, tiled=True)  143 us
    all_to_all x1, blocking collectives, per_device(): lax.all_to_all(filters, 'chan', split_axis=1, concat_axis=2, tiled=True)  18.7 us
    dot_general x9, matrix products, tap_backward(): jnp.einsum('oi,orc->irc', weights[tap_row * 3 + tap_col], source[:, 2 - t...  9.69 us
    all_to_all x1, starting transfers between devices, _keep_up_cubes(): lax.all_to_all(jnp.stack([values for _ in range(lax.axis_size(bus_axis))]...  7.26 us
    unnamed x11, local copies, waits for them, and re-layouts  7.03 us
    dot_general x9, matrix products, tap_forward(): jnp.einsum('oi,irc->orc', weights[tap_row * 3 + tap_col], source[:, tap_r...  6.25 us
  transfers between devices with their start and end apart: 4, of which 2 were waited for; matrix products, arithmetic and copies ran while one was open for 9% of the time, Pallas kernels for 0%

profile of v1, /device:TPU:90, one launch (start us, length us, event | category | flops | bytes accessed | tf_op | source)
XLA Modules:
  0.0 222.8 jit_solution(8628876053817600223)
XLA Ops:
  7.2 1.0 copy_bitcast_fusion.1
  8.2 1.9 collective-permute-start
  10.2 3.6 %collective-permute-start.1 = (bf16[2,32,1,512]{3,1,2,0:T(8,128)(2,1)S(1)}, bf16[2,32,1,512]{3,1,2,0:T(8,128)(2,1)S(1)}, u32[]{:S(2)}, u32[]{:S(2)}) collective-permute-start(bf16[2,32,1,512]{3,1,2,0:T(8,128)(2,1)S(1)} %get-tuple-element.18), channel_id=1, source_target_pairs={{16,0},{32,16},{48,32},{64,48},{80,64},{96,80},{112,96},{128,112},... | collective-permute-start | bytes 196616 | tf_op jit(solution)/shard_map/ppermute | solution.py:15
  13.8 1.9 collective-permute-done.1
  16.7 2.9 %copy.14 = bf16[9,512,32]{2,0,1:T(8,128)(2,1)S(1)} copy(bf16[9,512,32]{1,2,0:T(8,128)(2,1)} %param.5) | data formatting | bytes 589824 | tf_op args[1]
  19.6 1.3 reshape.56
  20.9 18.7 %all_to_all.20 = bf16[16,2,4608]{2,1,0:T(2,128)(2,1)S(1)} all-to-all(bf16[16,2,4608]{2,1,0:T(2,128)(2,1)S(1)} %reshape.56), channel_id=1, replica_groups=mesh['band'=32,'chan'=16] {'chan'}, dimensions={0} | all-to-all | bytes 589824 | tf_op jit(solution)/shard_map/all_to_all | solution.py:56
  39.5 2.4 %stack.15 = bf16[16,32,6,514]{3,1,2,0:T(8,128)(2,1)} broadcast(bf16[32,6,514]{2,0,1:T(8,128)(2,1)S(1)} %get-tuple-element.16), dimensions={1,2,3} | broadcast | bytes 3355392 | tf_op jit(solution)/shard_map/stack | solution.py:62
  42.0 7.3 %all-to-all-start = ((bf16[16,32,6,514]{3,1,2,0:T(8,128)(2,1)}), bf16[16,32,6,514]{3,1,2,0:T(8,128)(2,1)}, u32[]{:S(2)}, u32[]{:S(2)}) async-start(bf16[16,32,6,514]{3,1,2,0:T(8,128)(2,1)} %stack.15), calls=%async_computation | async-start | bytes 7864320 | tf_op jit(solution)/shard_map/all_to_all | solution.py:61
  49.2 1.4 reshape.57
  50.6 0.8 copy.21
  53.1 142.7 %all-gather.3.cloned.1.call-done = bf16[1,512,6,514]{3,1,2,0:T(8,128)(2,1)} async-done(((bf16[1,32,6,514]{3,1,2,0:T(8,128)(2,1)}), bf16[1,512,6,514]{3,1,2,0:T(8,128)(2,1)}) %all-gather.3.cloned.1.call-update) | async-done | bytes 3158032 | tf_op jit(solution)/shard_map/all_gather | solution.py:74
  195.9 2.2 fusion
  198.1 2.5 %fusion.10 = f32[4,512,32]{1,2,0:T(8,128)S(1)} fusion(bf16[512,6,514]{2,0,1:T(8,128)(2,1)} %bitcast.91, bf16[9,512,32]{1,2,0:T(8,128)(2,1)S(1)} %copy-done.1), kind=kOutput, calls=%fused_computation.10 | convolution fusion | flops 67108864 | bytes 2392064 | tf_op jit(solution)/shard_map/oi,orc->irc/dot_general | solution.py:38
  201.1 0.8 fusion.14
  201.9 0.8 fusion.2
  202.7 0.8 fusion.4
  203.9 0.8 fusion.8
  204.7 0.8 fusion.96
  206.3 2.6 %copy.13 = bf16[16,32,6,514]{3,1,0,2:T(8,128)(2,1)S(1)} copy(bf16[16,32,6,514]{3,1,2,0:T(8,128)(2,1)} %all-to-all-done) | data formatting | bytes 6316032 | tf_op jit(solution)/shard_map/all_to_all | solution.py:61
  209.4 0.8 fusion.30
  210.2 0.8 fusion.32
  211.0 0.8 fusion.26
  213.0 0.8 fusion.20
  (33 shorter events, 8.2 us)
Async XLA Ops:
  7.2 188.7 %all-gather.3.cloned.1.call-start = ((), (), s32[]{:S(2)}) async-start(), calls=%async_computation.2 | async-start | bytes 4177920 | tf_op jit(solution)/shard_map/all_gather | solution.py:74
  8.2 5.6 %collective-permute-start = (bf16[2,32,1,512]{3,1,2,0:T(8,128)(2,1)S(1)}, bf16[2,32,1,512]{3,1,2,0:T(8,128)(2,1)S(1)}, u32[]{:S(2)}, u32[]{:S(2)}) collective-permute-start(bf16[2,32,1,512]{3,1,2,0:T(8,128)(2,1)S(1)} %get-tuple-element.17), channel_id=1, source_target_pairs={{0,16},{16,32},{32,48},{48,64},{64,80},{80,96},{96,112},{112,128},... | collective-permute-start | bytes 196616 | tf_op jit(solution)/shard_map/ppermute | solution.py:14
  10.2 5.5 %collective-permute-start.1 = (bf16[2,32,1,512]{3,1,2,0:T(8,128)(2,1)S(1)}, bf16[2,32,1,512]{3,1,2,0:T(8,128)(2,1)S(1)}, u32[]{:S(2)}, u32[]{:S(2)}) collective-permute-start(bf16[2,32,1,512]{3,1,2,0:T(8,128)(2,1)S(1)} %get-tuple-element.18), channel_id=1, source_target_pairs={{16,0},{32,16},{48,32},{64,48},{80,64},{96,80},{112,96},{128,112},... | collective-permute-start | bytes 196616 | tf_op jit(solution)/shard_map/ppermute | solution.py:15
  42.0 7.3 %copy-start.2 = (bf16[32]{0:T(256)(128)(2,1)S(1)}, bf16[32]{0:T(256)(128)(2,1)}, u32[]{:S(2)}) copy-start(bf16[32]{0:T(256)(128)(2,1)} %param.6) | copy-start | bytes 196
  42.0 164.4 %all-to-all-start = ((bf16[16,32,6,514]{3,1,2,0:T(8,128)(2,1)}), bf16[16,32,6,514]{3,1,2,0:T(8,128)(2,1)}, u32[]{:S(2)}, u32[]{:S(2)}) async-start(bf16[16,32,6,514]{3,1,2,0:T(8,128)(2,1)} %stack.15), calls=%async_computation | async-start | bytes 7864320 | tf_op jit(solution)/shard_map/all_to_all | solution.py:61
  50.6 145.2 %copy-start.1 = (bf16[9,512,32]{1,2,0:T(8,128)(2,1)S(1)}, bf16[9,512,32]{1,2,0:T(8,128)(2,1)}, u32[]{:S(2)}) copy-start(bf16[9,512,32]{1,2,0:T(8,128)(2,1)} %param.5) | copy-start | bytes 884740
  195.9 4.7 %copy-start = (bf16[1,512,6,514]{3,1,2,0:T(8,128)(2,1)S(1)}, bf16[1,512,6,514]{3,1,2,0:T(8,128)(2,1)}, u32[]{:S(2)}) copy-start(bf16[1,512,6,514]{3,1,2,0:T(8,128)(2,1)} %all-gather.3.cloned.1.call-done) | copy-start | bytes 9474052
Sparse Core Ops, SparseCore 0:
  16.9 178.9 all-gather.2
